TPU v7x, 32 devices: a whole 2x2x4 slice. The times are simulated.
32 devices in a mesh: seg: 2 (over y), row: 4 (over x, core), col: 4 (over z).
Axes of the slice: x: 2, y: 2, z: 4, core: 2. Of those that a mesh axis runs over, the one named last changes fastest.
Arguments:
- raw_traces: bfloat16 [8192, 16, 256], P(('seg', 'row', 'col')), parts along dimension 0, may hold values from -6 to 6
- channel_pick: int32 [4096], P(('seg', 'row', 'col')), parts along dimension 0, may hold values from 0 to 4095, as said below
- clip_mask: int32 [4096, 16], P(('seg', 'row', 'col')), parts along dimension 0, may hold values 0 or 1
Outputs:
- correlations: bfloat16 [4096, 2048, 128], P(('seg', 'row'), 'col'), parts along dimension 0
There are 2 independent parts, one for each index of `seg`. A program takes and returns all parts, laid end to end along the dimension named above; each array names one. Nothing has to cross between parts.
Inputs may be any that keep to these rules, and one draw needn't show every extreme that they name: `channel_pick`: entry j is 2j or 2j+1; entry 0 is even and entry 2047 is odd.
All inputs are finite; a program needn't handle non-finite values. No bound on the sum of `clip_mask` on one device may be relied on, other than what follows from the above.
Results may differ from a plain program's by a relative error of at most 0.0057.
Values may be sent and summed in bfloat16 or wider, within the bound.
A program may use at most 576 MiB of HBM per device.

v0:
```python
import math

import jax
import jax.numpy as jnp
from jax import lax
from jax.sharding import PartitionSpec as P

L = 128


def broadcast(value, axis, source):
    kept = jnp.where(lax.axis_index(axis) == source, value, 0).astype(value.dtype)
    return lax.psum(kept, axis)


def whiten_block(picked, keep):
    samples = picked.shape[2]
    half = samples // 2
    pos = jnp.arange(samples, dtype=jnp.int32)
    freq = jnp.arange(1, half + 1, dtype=jnp.int32)
    phase = pos[:, None] * freq[None, :] % samples
    angle = phase.astype(jnp.float32) * (2.0 * math.pi / samples)
    table = jnp.concatenate([jnp.cos(angle), -jnp.sin(angle)], axis=1)
    flat = picked.astype(jnp.float32).reshape(-1, samples)
    spec = jnp.dot(flat, table, precision=lax.Precision.HIGHEST, preferred_element_type=jnp.float32)
    real_part = spec[:, :half]
    imag_part = spec[:, half:]
    power = real_part * real_part + imag_part * imag_part
    gap = jnp.abs(freq[:, None] - freq[None, :])
    band = jnp.where(gap <= 2, 0.2, 0.0).astype(jnp.float32)
    smooth = jnp.dot(
        power, band, precision=lax.Precision.HIGHEST, preferred_element_type=jnp.float32
    )
    denom = jnp.sqrt(smooth + 0.1 * jnp.mean(power, axis=1, keepdims=True) + 1e-06)
    weight = keep.reshape(-1, 1).astype(jnp.float32) / denom
    whitened = jnp.concatenate([real_part * weight, imag_part * weight], axis=1)
    return whitened.astype(jnp.bfloat16).reshape(picked.shape[0], picked.shape[1], samples)


def lag_tables(half, samples, lags, windows):
    freq = jnp.arange(1, half + 1, dtype=jnp.int32)
    shift = jnp.arange(lags, dtype=jnp.int32) - lags // 2
    phase = freq[:, None] * shift[None, :] % samples
    angle = phase.astype(jnp.float32) * (2.0 * math.pi / samples)
    scale = 1.0 / math.sqrt(windows * half)
    return (jnp.cos(angle) * scale, jnp.sin(angle) * scale)


def local(raw_traces, channel_pick, clip_mask):
    owned = channel_pick.shape[0]
    windows = raw_traces.shape[1]
    samples = raw_traces.shape[2]
    half = samples // 2
    paired = raw_traces.reshape(owned, 2, windows, samples)
    parity = (channel_pick % 2)[:, None, None]
    picked = jnp.where(parity == 1, paired[:, 1], paired[:, 0])
    diagonal = lax.axis_index("col")
    outgoing = whiten_block(picked, clip_mask)
    row_first, row_keep = (
        lax.all_gather(outgoing, "col", axis=0, tiled=True),
        lax.all_gather(clip_mask, "col", axis=0, tiled=True),
    )
    col_first, col_keep = (
        broadcast(row_first, "row", diagonal),
        broadcast(row_keep, "row", diagonal),
    )
    tile = row_first.shape[0]
    lags = L
    rotated = jnp.concatenate([-col_first[:, :, half:], col_first[:, :, :half]], axis=2)
    row_four = row_first.reshape(tile, windows, 2, half)
    col_four = col_first.reshape(tile, windows, 2, half)
    rot_four = rotated.reshape(tile, windows, 2, half)
    cross_re = jnp.einsum("iwpk,jwpk->ijk", row_four, col_four, preferred_element_type=jnp.float32)
    cross_im = jnp.einsum("iwpk,jwpk->ijk", row_four, rot_four, preferred_element_type=jnp.float32)
    cos_table, sin_table = lag_tables(half, samples, lags, windows)
    lagged = jnp.dot(
        cross_re.reshape(-1, half),
        cos_table,
        precision=lax.Precision.HIGHEST,
        preferred_element_type=jnp.float32,
    )
    lagged = lagged - jnp.dot(
        cross_im.reshape(-1, half),
        sin_table,
        precision=lax.Precision.HIGHEST,
        preferred_element_type=jnp.float32,
    )
    lagged = lagged.reshape(tile, tile, lags)
    row_ids = lax.axis_index("row") * tile + jnp.arange(tile, dtype=jnp.int32)
    col_ids = diagonal * tile + jnp.arange(tile, dtype=jnp.int32)
    same = row_ids[:, None] == col_ids[None, :]
    return jnp.where(same[:, :, None], 0.0, lagged).astype(jnp.bfloat16)


def solution(mesh):
    return jax.shard_map(
        local,
        mesh=mesh,
        in_specs=(
            P(("seg", "row", "col"), None, None),
            P(("seg", "row", "col")),
            P(("seg", "row", "col"), None),
        ),
        out_specs=P(("seg", "row"), "col", None),
        check_vma=False,
    )
```

profile of v0, /device:TPU:0, one launch (start us, length us, event | category | flops | bytes accessed | tf_op | source)
XLA Modules:
  0.0 1067.3 jit_solution(9108566769542848185)
XLA Ops:
  6.5 0.0 copy-start.5
  6.5 0.0 all-gather.2.cloned.1.call-start
  6.5 0.6 iota_add_fusion.2
  7.1 0.0 copy-start.2
  7.1 0.5 fusion.27
  7.7 1.7 fusion.53
  9.4 0.0 copy-done.5
  9.4 0.1 broadcast_in_dim.49
  9.5 0.1 broadcast_in_dim.50
  9.6 0.0 copy-start.1
  9.6 0.6 bitcast_select_fusion
  10.2 1.0 fusion.7
  11.2 0.3 fusion.11
  11.6 0.0 copy-done.1
  11.6 0.1 copy.4
  11.7 0.1 convert_element_type.31
  11.8 0.0 copy-done.2
  11.8 1.5 multiply_convert_fusion.1
  13.3 0.5 copy.5
  13.8 0.5 copy.6
  14.3 1.0 pad_maximum_fusion.1
  15.3 0.0 all-gather.2.cloned.1.call-update
  15.3 0.2 all-reduce.2.cloned.1.call-start
  15.6 83.2 %all-gather.2.cloned.1.call-done = bf16[512,16,256]{0,2,1:T(8,128)(2,1)} async-done(((bf16[128,16,256]{0,2,1:T(8,128)(2,1)}), bf16[512,16,256]{0,2,1:T(8,128)(2,1)}) %all-gather.2.cloned.1.call-update) | async-done | bytes 4194320 | tf_op jit(solution)/shard_map/all_gather | solution.py:60
  98.8 4.5 broadcast_select_fusion
  103.2 0.0 all-reduce.2.cloned.1.call-update
  103.3 0.9 broadcast_compare_fusion
  104.2 82.9 %all-reduce.2.cloned.1.call-done = bf16[512,16,256]{0,2,1:T(8,128)(2,1)} async-done(((bf16[512,16,256]{0,2,1:T(8,128)(2,1)}), bf16[512,16,256]{0,2,1:T(8,128)(2,1)}) %all-reduce.2.cloned.1.call-update) | async-done | bytes 4194320 | tf_op jit(solution)/shard_map/psum | solution.py:13
  187.1 48.9 %convolution_bitcast_fusion.1 = f32[512,512,128]{0,1,2:T(8,128)} fusion(bf16[512,16,2,128]{0,3,2,1:T(8,128)(2,1)} %bitcast.30, bf16[512,16,2,128]{0,3,2,1:T(8,128)(2,1)} %bitcast.28), kind=kOutput, calls=%fused_computation.3 | convolution fusion | flops 2147483648 | bytes 142606336 | tf_op jit(solution)/shard_map/iwpk,jwpk->ijk/dot_general | solution.py:73
  236.0 134.1 %copy.9 = f32[512,512,128]{2,1,0:T(8,128)} copy(f32[512,512,128]{0,1,2:T(8,128)} %convolution_bitcast_fusion.1) | data formatting | bytes 268435456 | tf_op jit(solution)/shard_map/iwpk,jwpk->ijk/transpose | solution.py:73
  370.1 2.5 slice_negate_fusion
  372.6 2.4 pad_maximum_fusion
  374.9 48.9 %convolution_bitcast_fusion = f32[512,512,128]{0,1,2:T(8,128)} fusion(bf16[512,16,2,128]{0,3,2,1:T(8,128)(2,1)} %bitcast.31, bf16[512,16,2,128]{0,3,2,1:T(8,128)(2,1)} %bitcast.29), kind=kOutput, calls=%fused_computation.2 | convolution fusion | flops 2147483648 | bytes 142606336 | tf_op jit(solution)/shard_map/iwpk,jwpk->ijk/dot_general | solution.py:74
  423.8 0.0 copy-start.3
  423.8 0.0 copy-start.4
  423.8 134.1 %copy.12 = f32[512,512,128]{2,1,0:T(8,128)} copy(f32[512,512,128]{0,1,2:T(8,128)} %convolution_bitcast_fusion) | data formatting | bytes 268435456 | tf_op jit(solution)/shard_map/iwpk,jwpk->ijk/transpose | solution.py:74
  557.9 0.0 copy-done.3
  557.9 0.0 copy-done.4
  557.9 224.6 %fusion.23 = f32[262144,128]{1,0:T(8,128)} fusion(f32[262144,128]{1,0:T(8,128)} %bitcast.10, s32[128]{0:T(128)S(1)} %copy-done.4, s32[128]{0:T(128)S(1)} %copy-done.3), kind=kOutput, calls=%fused_computation.46 | convolution fusion | flops 51539853312 | bytes 268436480 | tf_op jit(solution)/shard_map/dot_general | solution.py:76
  782.5 0.0 copy-start
  782.5 228.1 %convolution_subtract_fusion = bf16[262144,128]{1,0:T(8,128)(2,1)} fusion(f32[262144,128]{1,0:T(8,128)} %fusion.23, f32[262144,128]{1,0:T(8,128)} %bitcast.15, s32[128]{0:T(128)S(1)} %copy-done.4, s32[128]{0:T(128)S(1)} %copy-done.3), kind=kOutput, calls=%fused_computation | convolution fusion | flops 51606962176 | bytes 335545344 | tf_op jit(solution)/shard_map/dot_general | solution.py:82
  1010.6 0.0 copy-done
  1010.6 49.9 %select_convert_fusion = bf16[512,512,128]{2,1,0:T(8,128)(2,1)} fusion(bf16[512,512,128]{2,1,0:T(8,128)(2,1)} %bitcast.16, pred[512,512]{1,0:T(8,128)(4,1)S(1)} %copy-done), kind=kLoop, calls=%fused_computation.1 | loop fusion | flops 33554432 | bytes 134479872 | tf_op jit(solution)/shard_map/convert_element_type | solution.py:92
  (4 shorter events, 0.0 us)
Async XLA Ops:
  6.5 2.8 copy-start.5
  6.5 92.2 %all-gather.2.cloned.1.call-start = ((), (), s32[]{:S(2)}) async-start(), calls=%async_computation | async-start | bytes 5242880 | tf_op jit(solution)/shard_map/all_gather | solution.py:60
  7.1 4.7 copy-start.2
  9.6 2.0 copy-start.1
  15.3 171.8 %all-reduce.2.cloned.1.call-start = ((), (), s32[]{:S(2)}) async-start(), calls=%async_computation.1 | async-start | bytes 8388608 | tf_op jit(solution)/shard_map/psum | solution.py:13
  423.8 134.1 %copy-start.3 = (s32[128]{0:T(128)S(1)}, s32[128]{0:T(128)}, u32[]{:S(2)}) copy-start(s32[128]{0:T(128)} %copy-done.2) | copy-start | bytes 1540
  423.8 134.1 %copy-start.4 = (s32[128]{0:T(128)S(1)}, s32[128]{0:T(128)}, u32[]{:S(2)}) copy-start(s32[128]{0:T(128)} %get-tuple-element.13) | copy-start | bytes 1540
  782.5 228.1 %copy-start = (pred[512,512]{1,0:T(8,128)(4,1)S(1)}, pred[512,512]{1,0:T(8,128)(4,1)}, u32[]{:S(2)}) copy-start(pred[512,512]{1,0:T(8,128)(4,1)} %broadcast_compare_fusion) | copy-start | bytes 786436
Sparse Core Ops, SparseCore 0:
  15.4 83.2 all-gather.1
  103.4 83.6 all-reduce.1
where the time goes:
time: 1070 us
  matrix products  553 us (52%)
  local copies, waits for them, and re-layouts  271 us (25%)
  waiting for transfers between devices  166 us (16%)
  other arithmetic  63.3 us (6%)
  between operations  13.5 us (1%)
    dot_general x1, matrix products, local(): jnp.dot(cross_im.reshape(-1, half), sin_table, precision=lax.Precision.HI...  228 us
    dot_general x1, matrix products, local(): jnp.dot(cross_re.reshape(-1, half), cos_table, precision=lax.Precision.HI...  225 us
    transpose x1, local copies, waits for them, and re-layouts, local(): jnp.einsum('iwpk,jwpk->ijk', row_four, rot_four, preferred_element_type=j...  134 us
    transpose x1, local copies, waits for them, and re-layouts, local(): jnp.einsum('iwpk,jwpk->ijk', row_four, col_four, preferred_element_type=j...  134 us
    all_gather x1, waiting for transfers between devices, local(): lax.all_gather(outgoing, 'col', axis=0, tiled=True)  83.2 us
    psum x1, waiting for transfers between devices, broadcast(): return lax.psum(kept, axis)  82.9 us
    convert_element_type x1, other arithmetic, local(): return jnp.where(same[:, :, None], 0.0, lagged).astype(jnp.bfloat16)  49.9 us
    dot_general x1, matrix products, local(): jnp.einsum('iwpk,jwpk->ijk', row_four, rot_four, preferred_element_type=j...  48.9 us
  transfers between devices with their start and end apart: 2, of which 2 were waited for; matrix products, arithmetic and copies ran while one was open for 0% of the time, Pallas kernels for 0%

commit v1 on v0

v1 whole, which is shorter than its diff:
```python
import functools
import math

import jax
import jax.numpy as jnp
from jax import lax
from jax.experimental import pallas as pl
from jax.experimental.pallas import tpu as pltpu
from jax.sharding import PartitionSpec as P

L = 128
LANES = 128
PAD = 8
FLIP = True
UNROLL1 = 4
UNROLL2 = 4


def whiten_block(picked, keep):
    samples = picked.shape[2]
    half = samples // 2
    pos = jnp.arange(samples, dtype=jnp.int32)
    freq = jnp.arange(1, half + 1, dtype=jnp.int32)
    phase = pos[:, None] * freq[None, :] % samples
    angle = phase.astype(jnp.float32) * (2.0 * math.pi / samples)
    table = jnp.concatenate([jnp.cos(angle), -jnp.sin(angle)], axis=1)
    flat = picked.astype(jnp.float32).reshape(-1, samples)
    spec = jnp.dot(flat, table, precision=lax.Precision.HIGHEST, preferred_element_type=jnp.float32)
    real_part = spec[:, :half]
    imag_part = spec[:, half:]
    power = real_part * real_part + imag_part * imag_part
    gap = jnp.abs(freq[:, None] - freq[None, :])
    band = jnp.where(gap <= 2, 0.2, 0.0).astype(jnp.float32)
    smooth = jnp.dot(
        power, band, precision=lax.Precision.HIGHEST, preferred_element_type=jnp.float32
    )
    denom = jnp.sqrt(smooth + 0.1 * jnp.mean(power, axis=1, keepdims=True) + 1e-06)
    weight = keep.reshape(-1, 1).astype(jnp.float32) / denom
    whitened = jnp.concatenate([real_part * weight, imag_part * weight], axis=1)
    return whitened.astype(jnp.bfloat16).reshape(picked.shape[0], picked.shape[1], samples)


def lag_table(half, samples, lags, windows):
    freq = jnp.arange(1, half + 1, dtype=jnp.int32)
    shift = jnp.arange(lags, dtype=jnp.int32) - lags // 2
    phase = freq[:, None] * shift[None, :] % samples
    angle = phase.astype(jnp.float32) * (2.0 * math.pi / samples)
    scale = 1.0 / math.sqrt(windows * half)
    both = jnp.concatenate([jnp.cos(angle) * scale, -jnp.sin(angle) * scale], axis=0)
    return both.astype(jnp.bfloat16)


def pair_kernel(offs_ref, first_ref, second_ref, table_ref, out_ref, cross_ref):
    groups, half, depth, wide = second_ref.shape
    rows = first_ref.shape[-1]
    both = 2 * half
    stride = both + PAD
    windows = depth // 2

    def spectra(k, carry):
        a = first_ref[k]
        turned = jnp.concatenate([a[windows:], -a[:windows]], axis=0)
        b = jnp.concatenate([second_ref[g, k] for g in range(groups)], axis=1)
        for part, lhs in enumerate((a, turned)):
            res = lax.dot_general(
                lhs, b, (((0,), (0,)), ((), ())), preferred_element_type=jnp.float32
            )
            for g in range(groups):
                cross_ref[g, pl.ds(part * half + k, rows, stride=stride), :] = res[
                    :, g * wide : (g + 1) * wide
                ]
        return carry

    lax.fori_loop(0, half, spectra, 0, unroll=UNROLL1)

    row0 = offs_ref[0] + pl.program_id(0) * rows
    col0 = offs_ref[1] + pl.program_id(1) * (groups * wide)
    lags = table_ref.shape[0] if FLIP else table_ref.shape[1]
    place = lax.broadcasted_iota(jnp.int32, (groups * wide, lags), 0) + (col0 - row0)

    def lagged(i, carry):
        start = pl.multiple_of(i * stride, 8)
        x = jnp.concatenate(
            [cross_ref[g, pl.ds(start, both), :].astype(jnp.bfloat16) for g in range(groups)],
            axis=1,
        )
        if FLIP:
            res = jnp.dot(table_ref[...], x, preferred_element_type=jnp.float32).T
        else:
            res = lax.dot_general(
                x, table_ref[...], (((0,), (0,)), ((), ())), preferred_element_type=jnp.float32
            )
        out_ref[i] = jnp.where(place == i, 0.0, res).astype(out_ref.dtype)
        return carry

    lax.fori_loop(0, rows, lagged, 0, unroll=UNROLL2)


def correlate(first, second, table, offs):
    na, half, depth, rows = first.shape
    nb, _, _, wide = second.shape
    groups = 2 if nb % 2 == 0 else 1
    lags = table.shape[1]
    if FLIP:
        table = table.T
    spec = pltpu.PrefetchScalarGridSpec(
        num_scalar_prefetch=1,
        grid=(na, nb // groups),
        in_specs=[
            pl.BlockSpec((None, half, depth, rows), lambda i, j, o: (i, 0, 0, 0)),
            pl.BlockSpec((groups, half, depth, wide), lambda i, j, o: (j, 0, 0, 0)),
            pl.BlockSpec(table.shape, lambda i, j, o: (0, 0)),
        ],
        out_specs=pl.BlockSpec((rows, groups * wide, lags), lambda i, j, o: (i, j, 0)),
        scratch_shapes=[pltpu.VMEM((groups, rows * (2 * half + PAD), wide), jnp.float32)],
    )
    return pl.pallas_call(
        pair_kernel,
        grid_spec=spec,
        out_shape=jax.ShapeDtypeStruct((na * rows, nb * wide, lags), jnp.bfloat16),
        compiler_params=pltpu.CompilerParams(
            dimension_semantics=("arbitrary", "arbitrary"), vmem_limit_bytes=60 * 1024 * 1024
        ),
        name="pair_correlations",
    )(offs, first, second, table)


def by_lanes(parts):
    count, half, depth, owned = parts.shape
    if owned == LANES:
        return parts
    whole = parts.transpose(1, 2, 0, 3).reshape(half, depth, count * owned)
    lanes = math.gcd(LANES, count * owned)
    return whole.reshape(half, depth, -1, lanes).transpose(2, 0, 1, 3)


def local(rows, cols, raw_traces, channel_pick, clip_mask):
    owned = channel_pick.shape[0]
    windows = raw_traces.shape[1]
    samples = raw_traces.shape[2]
    half = samples // 2
    paired = raw_traces.reshape(owned, 2, windows, samples)
    parity = (channel_pick % 2)[:, None, None]
    picked = jnp.where(parity == 1, paired[:, 1], paired[:, 0])
    outgoing = whiten_block(picked, clip_mask)
    outgoing = outgoing.reshape(owned, windows, 2, half).transpose(3, 2, 1, 0)
    outgoing = outgoing.reshape(half, 2 * windows, owned)
    across = lax.ppermute(
        outgoing,
        ("row", "col"),
        [(c * cols + r, r * cols + c) for r in range(rows) for c in range(cols)],
    )
    second = lax.all_gather(across, "row", axis=0)
    first = lax.all_gather(outgoing, "col", axis=0)
    tile = owned * cols
    offs = jnp.stack([lax.axis_index("row") * tile, lax.axis_index("col") * tile])
    table = lag_table(half, samples, L, windows)
    return correlate(by_lanes(first), by_lanes(second), table, offs.astype(jnp.int32))


def solution(mesh):
    rows, cols = mesh.shape["row"], mesh.shape["col"]
    return jax.shard_map(
        functools.partial(local, rows, cols),
        mesh=mesh,
        in_specs=(
            P(("seg", "row", "col"), None, None),
            P(("seg", "row", "col")),
            P(("seg", "row", "col"), None),
        ),
        out_specs=P(("seg", "row"), "col", None),
        check_vma=False,
    )
```

time: 1070 us -> 387 us (0.36)
  matrix products: 553 us -> 2.49 us
  local copies, waits for them, and re-layouts: 271 us -> 6.18 us
  Pallas kernels: 0 us -> 207 us
  other arithmetic: 63.3 us -> 4.36 us
  waiting for transfers between devices: 166 us -> 152 us
    dot_general x4 -> x0, matrix products: 550 us -> none  [the longest x1 228 us: local(): jnp.dot(cross_im.reshape(-1, half), sin_table, precision=lax.Precision.HI...]
    transpose x2 -> x1, local copies, waits for them, and re-layouts: 268 us -> 2.23 us  [local(): outgoing = outgoing.reshape(owned, windows, 2, half).transpose(3, 2, 1, 0)]
    pallas_call x0 -> x1, Pallas kernels: none -> 207 us  [correlate(): pl.pallas_call(pair_kernel, grid_spec=spec, out_shape=jax.ShapeDtypeStruc...]
    psum x1 -> x0, waiting for transfers between devices: 82.9 us -> none  [broadcast(): return lax.psum(kept, axis)]
    all_gather x1 -> x2, waiting for transfers between devices: 83.2 us -> 152 us  [the longest x1 117 us: local(): first = lax.all_gather(outgoing, 'col', axis=0)]
    convert_element_type x1 -> x0, other arithmetic: 49.9 us -> none  [local(): return jnp.where(same[:, :, None], 0.0, lagged).astype(jnp.bfloat16)]
  transfers between devices with their start and end apart: 2 -> 3, of which waited for: 2 -> 2; matrix products, arithmetic and copies ran while one was open for 0% -> 0% of each run, Pallas kernels for 0% -> 0%
where the time goes in v1:
time: 387 us
  Pallas kernels  207 us (53%)
  waiting for transfers between devices  152 us (39%)
  between operations  13.5 us (3%)
  local copies, waits for them, and re-layouts  6.18 us (2%)
  other arithmetic  4.36 us (1%)
    pallas_call x1, Pallas kernels, correlate(): pl.pallas_call(pair_kernel, grid_spec=spec, out_shape=jax.ShapeDtypeStruc...  207 us
    all_gather x1, waiting for transfers between devices, local(): first = lax.all_gather(outgoing, 'col', axis=0)  117 us
    all_gather x1, waiting for transfers between devices, local(): second = lax.all_gather(across, 'row', axis=0)  35.2 us
  transfers between devices with their start and end apart: 3, of which 2 were waited for; matrix products, arithmetic and copies ran while one was open for 0% of the time, Pallas kernels for 0%

profile of v1, /device:TPU:0, one launch (start us, length us, event | category | flops | bytes accessed | tf_op | source)
XLA Modules:
  0.0 386.9 jit_solution(4852198247731417943)
XLA Ops:
  6.5 0.0 all-gather.4.cloned.1.call-start
  6.5 0.7 fusion.24
  7.2 0.7 convert_element_type.29
  7.9 0.1 broadcast_in_dim.28
  8.0 0.1 broadcast_in_dim.29
  8.1 0.1 copy.15
  8.2 0.1 convert_element_type.30
  8.3 0.5 fusion.18
  8.8 1.7 fusion.30
  10.5 0.6 bitcast_select_fusion
  11.1 1.0 fusion.3
  12.2 0.2 fusion.7
  12.4 1.4 multiply_convert_fusion.1
  13.8 0.1 pad_maximum_fusion
  13.9 0.5 copy.16
  14.4 0.3 convert_element_type.31
  14.7 2.2 copy.17
  17.0 0.0 all-gather.4.cloned.1.call-update
  17.0 0.0 all-gather.6.cloned.1.call-start
  17.0 1.9 collective-permute-start
  18.9 0.0 collective-permute-done
  18.9 0.0 copy-start
  18.9 1.1 copy-done
  20.0 0.0 all-gather.6.cloned.1.call-update
  20.0 0.6 pad_add_fusion.offs_ref
  20.6 0.4 multiply_convert_fusion.3
  21.0 0.6 maximum_bitcast_fusion.table_ref
  21.6 116.6 %all-gather.4.cloned.1.call-done.first_ref = bf16[4,128,32,128]{3,2,1,0:T(8,128)(2,1)} async-done(((bf16[1,128,32,128]{3,2,1,0:T(8,128)(2,1)}), bf16[4,128,32,128]{3,2,1,0:T(8,128)(2,1)}) %all-gather.4.cloned.1.call-update) | async-done | bytes 4194320 | tf_op jit(solution)/shard_map/all_gather | solution.py:154
  138.2 35.2 %all-gather.6.cloned.1.call-done = bf16[512,32,128]{2,1,0:T(8,128)(2,1)} async-done(((bf16[128,32,128]{2,1,0:T(8,128)(2,1)}), bf16[512,32,128]{2,1,0:T(8,128)(2,1)}) %all-gather.6.cloned.1.call-update) | async-done | bytes 4194320 | tf_op jit(solution)/shard_map/all_gather | solution.py:153
  173.5 206.6 %pair_correlations.1 = bf16[512,512,128]{2,1,0:T(8,128)(2,1)} custom-call(s32[2]{0:T(128)} %pad_add_fusion.offs_ref, bf16[4,128,32,128]{3,2,1,0:T(8,128)(2,1)} %all-gather.4.cloned.1.call-done.first_ref, bf16[4,128,32,128]{3,2,1,0:T(8,128)(2,1)} %bitcast.14, bf16[128,256]{1,0:T(8,128)(2,1)} %maximum_bitcast_fusion.table_ref), custom_call_target="tpu_custom_call" | custom-call | tf_op jit(solution)/shard_map/pair_correlations/pallas_call | solution.py:117
  (2 shorter events, 0.0 us)
Async XLA Ops:
  6.5 131.7 %all-gather.4.cloned.1.call-start = ((), (), s32[]{:S(2)}) async-start(), calls=%async_computation | async-start | bytes 5242880 | tf_op jit(solution)/shard_map/all_gather | solution.py:154
  17.0 156.5 %all-gather.6.cloned.1.call-start = ((), (), s32[]{:S(2)}) async-start(), calls=%async_computation.1 | async-start | bytes 5242880 | tf_op jit(solution)/shard_map/all_gather | solution.py:153
  17.0 1.9 collective-permute-start
  18.9 1.1 copy-start
Sparse Core Ops, SparseCore 0:
  17.1 121.0 all-gather.3
  139.8 33.6 all-gather.5

commit v2 on v1

--- a/solution.py
+++ b/solution.py
@@ -11,7 +11,6 @@
 L = 128
 LANES = 128
 PAD = 8
-FLIP = True
 UNROLL1 = 4
 UNROLL2 = 4
 
@@ -50,17 +49,20 @@
     return both.astype(jnp.bfloat16)
 
 
-def pair_kernel(offs_ref, first_ref, second_ref, table_ref, out_ref, cross_ref):
-    groups, half, depth, wide = second_ref.shape
-    rows = first_ref.shape[-1]
+def pair_kernel(groups, offs_ref, first_ref, *refs):
+    second_refs = refs[:groups]
+    table_ref, out_ref, cross_ref = refs[groups], refs[-2], refs[-1]
+    half, depth, rows = first_ref.shape
+    wide = second_refs[0].shape[-1]
     both = 2 * half
     stride = both + PAD
     windows = depth // 2
+    chunk = out_ref.shape[0]
 
     def spectra(k, carry):
         a = first_ref[k]
         turned = jnp.concatenate([a[windows:], -a[:windows]], axis=0)
-        b = jnp.concatenate([second_ref[g, k] for g in range(groups)], axis=1)
+        b = jnp.concatenate([ref[k] for ref in second_refs], axis=1)
         for part, lhs in enumerate((a, turned)):
             res = lax.dot_general(
                 lhs, b, (((0,), (0,)), ((), ())), preferred_element_type=jnp.float32
@@ -71,64 +73,77 @@
                 ]
         return carry
 
-    lax.fori_loop(0, half, spectra, 0, unroll=UNROLL1)
-
-    row0 = offs_ref[0] + pl.program_id(0) * rows
-    col0 = offs_ref[1] + pl.program_id(1) * (groups * wide)
-    lags = table_ref.shape[0] if FLIP else table_ref.shape[1]
-    place = lax.broadcasted_iota(jnp.int32, (groups * wide, lags), 0) + (col0 - row0)
+    @pl.when(pl.program_id(0) == 0)
+    def _():
+        lax.fori_loop(0, half, spectra, 0, unroll=UNROLL1)
+
+    base = pl.program_id(0) * chunk
+    swap = offs_ref[2]
+    lags = table_ref.shape[0]
+    gap = offs_ref[3] - base
+    place = lax.broadcasted_iota(jnp.int32, (wide, lags), 0) + gap
+    halves = [swap * wide, (1 - swap) * wide] if groups == 2 else [0]
 
     def lagged(i, carry):
-        start = pl.multiple_of(i * stride, 8)
+        start = pl.multiple_of((base + i) * stride, 8)
         x = jnp.concatenate(
             [cross_ref[g, pl.ds(start, both), :].astype(jnp.bfloat16) for g in range(groups)],
             axis=1,
         )
-        if FLIP:
-            res = jnp.dot(table_ref[...], x, preferred_element_type=jnp.float32).T
-        else:
-            res = lax.dot_general(
-                x, table_ref[...], (((0,), (0,)), ((), ())), preferred_element_type=jnp.float32
-            )
-        out_ref[i] = jnp.where(place == i, 0.0, res).astype(out_ref.dtype)
+        res = jnp.dot(table_ref[...], x, preferred_element_type=jnp.float32).T
+        for g in range(groups):
+            at = halves[g]
+            piece = jnp.where(place + at == i, 0.0, res[g * wide : (g + 1) * wide])
+            if groups == 2:
+                at = pl.multiple_of(at, wide)
+            out_ref[i, pl.ds(at, wide), :] = piece.astype(out_ref.dtype)
         return carry
 
-    lax.fori_loop(0, rows, lagged, 0, unroll=UNROLL2)
-
-
-def correlate(first, second, table, offs):
-    na, half, depth, rows = first.shape
-    nb, _, _, wide = second.shape
-    groups = 2 if nb % 2 == 0 else 1
-    lags = table.shape[1]
-    if FLIP:
-        table = table.T
+    lax.fori_loop(0, chunk, lagged, 0, unroll=UNROLL2)
+
+
+def correlate(prev, first, seconds, table, offs, shape):
+    half, depth, rows = first.shape
+    wide = seconds[0].shape[-1]
+    groups = len(seconds)
+    lags = table.shape[0]
+    steps = 4 if rows % 4 == 0 else 1
+    in_specs = [pl.BlockSpec((half, depth, rows), lambda i, o: (0, 0, 0))]
+    in_specs += [pl.BlockSpec((half, depth, wide), lambda i, o: (0, 0, 0))] * groups
+    in_specs += [pl.BlockSpec(table.shape, lambda i, o: (0, 0))]
+    args = [offs, first, *seconds, table]
+    aliases = {}
+    if prev is not None:
+        aliases = {len(args): 0}
+        in_specs.append(pl.BlockSpec(memory_space=pl.ANY))
+        args.append(prev)
     spec = pltpu.PrefetchScalarGridSpec(
         num_scalar_prefetch=1,
-        grid=(na, nb // groups),
-        in_specs=[
-            pl.BlockSpec((None, half, depth, rows), lambda i, j, o: (i, 0, 0, 0)),
-            pl.BlockSpec((groups, half, depth, wide), lambda i, j, o: (j, 0, 0, 0)),
-            pl.BlockSpec(table.shape, lambda i, j, o: (0, 0)),
-        ],
-        out_specs=pl.BlockSpec((rows, groups * wide, lags), lambda i, j, o: (i, j, 0)),
+        grid=(steps,),
+        in_specs=in_specs,
+        out_specs=pl.BlockSpec(
+            (rows // steps, groups * wide, lags), lambda i, o: (o[0] * steps + i, o[1], 0)
+        ),
         scratch_shapes=[pltpu.VMEM((groups, rows * (2 * half + PAD), wide), jnp.float32)],
     )
+    flops = 2 * rows * groups * wide * 2 * half * (depth + lags)
     return pl.pallas_call(
-        pair_kernel,
+        functools.partial(pair_kernel, groups),
         grid_spec=spec,
-        out_shape=jax.ShapeDtypeStruct((na * rows, nb * wide, lags), jnp.bfloat16),
+        out_shape=jax.ShapeDtypeStruct(shape, jnp.bfloat16),
+        input_output_aliases=aliases,
+        cost_estimate=pl.CostEstimate(
+            flops=8 * flops, bytes_accessed=2 * rows * groups * wide * lags, transcendentals=0
+        ),
         compiler_params=pltpu.CompilerParams(
-            dimension_semantics=("arbitrary", "arbitrary"), vmem_limit_bytes=60 * 1024 * 1024
+            dimension_semantics=("arbitrary",), vmem_limit_bytes=60 * 1024 * 1024
         ),
         name="pair_correlations",
-    )(offs, first, second, table)
+    )(*args)
 
 
 def by_lanes(parts):
     count, half, depth, owned = parts.shape
-    if owned == LANES:
-        return parts
     whole = parts.transpose(1, 2, 0, 3).reshape(half, depth, count * owned)
     lanes = math.gcd(LANES, count * owned)
     return whole.reshape(half, depth, -1, lanes).transpose(2, 0, 1, 3)
@@ -150,12 +165,61 @@
         ("row", "col"),
         [(c * cols + r, r * cols + c) for r in range(rows) for c in range(cols)],
     )
-    second = lax.all_gather(across, "row", axis=0)
-    first = lax.all_gather(outgoing, "col", axis=0)
     tile = owned * cols
-    offs = jnp.stack([lax.axis_index("row") * tile, lax.axis_index("col") * tile])
-    table = lag_table(half, samples, L, windows)
-    return correlate(by_lanes(first), by_lanes(second), table, offs.astype(jnp.int32))
+    shape = (tile, tile, L)
+    row, col = lax.axis_index("row"), lax.axis_index("col")
+    ahead = (col - row) * tile
+    table = lag_table(half, samples, L, windows).T
+    prev = None
+
+    def offsets(place, pair, swap, wide, lanes):
+        gap = ahead + pair * wide - place * lanes
+        return jnp.stack([jnp.int32(v) for v in (place, pair, swap, gap)])
+
+    if owned != LANES or rows & (rows - 1) or rows < 2:
+        firsts = by_lanes(lax.all_gather(outgoing, "col", axis=0))
+        seconds = by_lanes(lax.all_gather(across, "row", axis=0))
+        lanes = firsts.shape[-1]
+        for i in range(firsts.shape[0]):
+            for j in range(seconds.shape[0]):
+                offs = offsets(i, j, 0, lanes, lanes)
+                prev = correlate(prev, firsts[i], [seconds[j]], table, offs, shape)
+        return prev
+
+    def flipped(value, bit):
+        return lax.ppermute(value, "row", [(r, r ^ bit) for r in range(rows)])
+
+    def hop(value):
+        return lax.ppermute(value, "col", [(c, (c + 1) % cols) for c in range(cols)])
+
+    pairs = {0: (across, flipped(across, 1))}
+    held, _ = lax.optimization_barrier((outgoing, across))
+    firsts = {0: outgoing, 1: hop(held)} if cols > 1 else {0: outgoing}
+    fars = {p: flipped(across, 2 * p) for p in range(1, rows // 2)}
+    order = [(s, p) for s in range(cols) for p in range(rows // 2)]
+    order.sort(key=lambda sp: (max(sp[0] // 2, sp[1]), sp[0] // 2, sp[1], sp[0]))
+    ready = 1
+    for step, (s, p) in enumerate(order):
+        if step > 0:
+            if p in fars and p not in pairs or step == 1 and fars:
+                for q in [q for q in fars if q not in pairs][:1]:
+                    prev, far = lax.optimization_barrier((prev, fars[q]))
+                    pairs[q] = (far, flipped(far, 1))
+            while p not in pairs:
+                q = len(pairs)
+                pairs[q] = (fars[q], flipped(fars[q], 1))
+            if ready + 1 < cols and (step % 2 == 1 or s > ready):
+                prev, last = lax.optimization_barrier((prev, firsts[ready]))
+                ready += 1
+                firsts[ready] = hop(last)
+            while s > ready:
+                ready += 1
+                firsts[ready] = hop(firsts[ready - 1])
+        place = (col - s) % cols
+        other = row ^ (2 * p)
+        offs = offsets(place, other // 2, other % 2, 2 * owned, owned)
+        prev = correlate(prev, firsts[s], pairs[p], table, offs, shape)
+    return prev
 
 
 def solution(mesh):

time: 387 us -> 309 us (0.80)
  waiting for transfers between devices: 152 us -> 0.02 us
  starting transfers between devices: 1.93 us -> 57.1 us
  Pallas kernels: 207 us -> 234 us
  between operations: 13.5 us -> 0.15 us
    all_gather x2 -> x0, waiting for transfers between devices: 152 us -> none  [the longest x1 117 us: local(): first = lax.all_gather(outgoing, 'col', axis=0)]
    ppermute x0 -> x6, starting transfers between devices: none -> 55.2 us  [the longest x3 53.3 us: flipped(): return lax.ppermute(value, 'row', [(r, r ^ bit) for r in range(rows)])]
    pallas_call x1 -> x8, Pallas kernels: 207 us -> 234 us  [correlate(): pl.pallas_call(functools.partial(pair_kernel, groups), grid_spec=spec, ou...]
  transfers between devices with their start and end apart: 3 -> 7, of which waited for: 2 -> 0; matrix products, arithmetic and copies ran while one was open for 0% -> 2% of each run, Pallas kernels for 0% -> 48%
where the time goes in v2:
time: 309 us; the launch traced here: 308 us
  Pallas kernels  234 us (76%)
  starting transfers between devices  57.1 us (18%)
  local copies, waits for them, and re-layouts  8.14 us (3%)
  other arithmetic  6.19 us (2%)
    pallas_call x8, Pallas kernels, correlate(): pl.pallas_call(functools.partial(pair_kernel, groups), grid_spec=spec, ou...  234 us
    ppermute x3, starting transfers between devices, flipped(): return lax.ppermute(value, 'row', [(r, r ^ bit) for r in range(rows)])  53.3 us
  transfers between devices with their start and end apart: 7, of which 0 were waited for; matrix products, arithmetic and copies ran while one was open for 2% of the time, Pallas kernels for 48%

profile of v2, /device:TPU:0, one launch (start us, length us, event | category | flops | bytes accessed | tf_op | source)
XLA Modules:
  0.0 308.4 jit_solution(11799548802212579770)
XLA Ops:
  0.0 0.5 fusion.18
  0.5 0.0 copy-start.7
  0.6 1.7 fusion.30
  2.3 0.1 broadcast_in_dim.28
  2.4 0.1 broadcast_in_dim.29
  2.5 0.6 bitcast_select_fusion
  3.1 0.0 copy-start.6
  3.1 1.0 fusion.3
  4.1 0.2 fusion.7
  4.3 0.1 copy.12
  4.4 0.1 convert_element_type.30
  4.5 1.4 multiply_convert_fusion.1
  5.9 0.1 pad_maximum_fusion
  6.0 0.5 copy.13
  6.6 0.3 convert_element_type.31
  6.9 2.3 copy.14
  9.2 1.9 collective-permute-start
  11.0 0.0 collective-permute-done.refs_0_
  11.0 24.4 %collective-permute-start.1 = (bf16[128,32,128]{2,1,0:T(8,128)(2,1)S(1)}, bf16[128,32,128]{2,1,0:T(8,128)(2,1)S(1)}, u32[]{:S(2)}, u32[]{:S(2)}) collective-permute-start(bf16[128,32,128]{2,1,0:T(8,128)(2,1)S(1)} %collective-permute-done.refs_0_), channel_id=1, source_target_pairs={{0,4},{4,0},{8,12},{12,8},{1,5},{5,1},{9,13},{13,9},{2,6},{6,2},{1... | collective-permute-start | bytes 3145736 | tf_op jit(solution)/shard_map/ppermute | solution.py:190
  35.4 0.6 pad_add_fusion.2.offs_ref
  36.0 0.6 pad_add_fusion.3.offs_ref
  36.6 0.6 pad_add_fusion.6.offs_ref
  37.2 0.7 pad_add_fusion.5.offs_ref
  37.9 0.7 pad_add_fusion.1
  38.6 0.7 pad_add_fusion
  39.2 0.3 multiply_convert_fusion.3
  39.6 0.6 maximum_bitcast_fusion.refs_2_
  40.2 0.0 collective-permute-start.4
  40.2 28.8 %collective-permute-start.2 = (bf16[128,32,128]{2,1,0:T(8,128)(2,1)S(1)}, bf16[128,32,128]{2,1,0:T(8,128)(2,1)S(1)}, u32[]{:S(2)}, u32[]{:S(2)}) collective-permute-start(bf16[128,32,128]{2,1,0:T(8,128)(2,1)S(1)} %collective-permute-done.refs_0_), channel_id=1, source_target_pairs={{0,8},{4,12},{8,0},{12,4},{1,9},{5,13},{9,1},{13,5},{2,10},{6,14},... | collective-permute-start | bytes 3145736 | tf_op jit(solution)/shard_map/ppermute | solution.py:190
  69.1 0.0 collective-permute-done.1.refs_1_
  69.1 1.0 copy-done.3
  70.0 29.3 %pair_correlations.8.refs_3_ = bf16[512,512,128]{2,1,0:T(8,128)(2,1)} custom-call(s32[4]{0:T(128)} %pad_add_fusion.2.offs_ref, bf16[128,32,128]{2,1,0:T(8,128)(2,1)} %bitcast.10.first_ref, bf16[128,32,128]{2,1,0:T(8,128)(2,1)} %copy-done.2, bf16[128,32,128]{2,1,0:T(8,128)(2,1)} %copy-done.3, bf16[128,256]{1,0:T(8,128)(2,1)} %maximum_bitcast_fusion.refs_2_), custom_call_target="tpu_custom_call" | custom-call | flops 21474836480 | bytes 8388608 | tf_op jit(solution)/shard_map/pair_correlations/pallas_call | solution.py:130
  99.3 0.0 collective-permute-done.2.refs_0_
  99.4 0.0 collective-permute-done.4.first_ref
  99.4 0.1 collective-permute-start.3
  99.4 0.1 collective-permute-start.5
  99.6 29.3 %pair_correlations.9.refs_3_ = bf16[512,512,128]{2,1,0:T(8,128)(2,1)} custom-call(s32[4]{0:T(128)} %pad_add_fusion.3.offs_ref, bf16[128,32,128]{2,1,0:T(8,128)(2,1)} %collective-permute-done.4.first_ref, bf16[128,32,128]{2,1,0:T(8,128)(2,1)} %copy-done.2, bf16[128,32,128]{2,1,0:T(8,128)(2,1)} %copy-done.3, ...), custom_call_target="tpu_custom_call", output_to_operand_aliasing={{}: (5, {})} | custom-call | flops 21474836480 | bytes 8388608 | tf_op jit(solution)/shard_map/pair_correlations/pallas_call | solution.py:130
  128.9 0.0 collective-permute-done.3.refs_1_
  128.9 1.0 copy-done.1
  129.9 29.3 %pair_correlations.10.refs_3_ = bf16[512,512,128]{2,1,0:T(8,128)(2,1)} custom-call(s32[4]{0:T(128)} %get-tuple-element.29.offs_ref, bf16[128,32,128]{2,1,0:T(8,128)(2,1)} %bitcast.10.first_ref, bf16[128,32,128]{2,1,0:T(8,128)(2,1)} %copy-done, bf16[128,32,128]{2,1,0:T(8,128)(2,1)} %copy-done.1, ...), custom_call_target="tpu_custom_call", output_to_operand_aliasing={{}: (5, {})} | custom-call | flops 21474836480 | bytes 8388608 | tf_op jit(solution)/shard_map/pair_correlations/pallas_call | solution.py:130
  159.1 0.0 collective-permute-done.5.first_ref
  159.1 1.8 collective-permute-start.6
  160.9 29.3 %pair_correlations.11.refs_3_ = bf16[512,512,128]{2,1,0:T(8,128)(2,1)} custom-call(s32[4]{0:T(128)} %get-tuple-element.30.offs_ref, bf16[128,32,128]{2,1,0:T(8,128)(2,1)} %collective-permute-done.4.first_ref, bf16[128,32,128]{2,1,0:T(8,128)(2,1)} %copy-done, bf16[128,32,128]{2,1,0:T(8,128)(2,1)} %copy-done.1, ...), custom_call_target="tpu_custom_call", output_to_operand_aliasing={{}: (5, {})} | custom-call | flops 21474836480 | bytes 8388608 | tf_op jit(solution)/shard_map/pair_correlations/pallas_call | solution.py:130
  190.2 29.3 %pair_correlations.12.refs_3_ = bf16[512,512,128]{2,1,0:T(8,128)(2,1)} custom-call(s32[4]{0:T(128)} %pad_add_fusion.6.offs_ref, bf16[128,32,128]{2,1,0:T(8,128)(2,1)} %copy-done.4, bf16[128,32,128]{2,1,0:T(8,128)(2,1)} %copy-done.2, bf16[128,32,128]{2,1,0:T(8,128)(2,1)} %copy-done.3, ...), custom_call_target="tpu_custom_call", output_to_operand_aliasing={{}: (5, {})} | custom-call | flops 21474836480 | bytes 8388608 | tf_op jit(solution)/shard_map/pair_correlations/pallas_call | solution.py:130
  219.5 1.0 copy-done.5
  220.5 29.3 %pair_correlations.13.refs_3_ = bf16[512,512,128]{2,1,0:T(8,128)(2,1)} custom-call(s32[4]{0:T(128)} %pad_add_fusion.5.offs_ref, bf16[128,32,128]{2,1,0:T(8,128)(2,1)} %copy-done.5, bf16[128,32,128]{2,1,0:T(8,128)(2,1)} %copy-done.2, bf16[128,32,128]{2,1,0:T(8,128)(2,1)} %copy-done.3, ...), custom_call_target="tpu_custom_call", output_to_operand_aliasing={{}: (5, {})} | custom-call | flops 21474836480 | bytes 8388608 | tf_op jit(solution)/shard_map/pair_correlations/pallas_call | solution.py:130
  249.8 29.3 %pair_correlations.14.refs_3_ = bf16[512,512,128]{2,1,0:T(8,128)(2,1)} custom-call(s32[4]{0:T(128)} %get-tuple-element.28.offs_ref, bf16[128,32,128]{2,1,0:T(8,128)(2,1)} %copy-done.4, bf16[128,32,128]{2,1,0:T(8,128)(2,1)} %copy-done, bf16[128,32,128]{2,1,0:T(8,128)(2,1)} %copy-done.1, ...), custom_call_target="tpu_custom_call", output_to_operand_aliasing={{}: (5, {})} | custom-call | flops 21474836480 | bytes 8388608 | tf_op jit(solution)/shard_map/pair_correlations/pallas_call | solution.py:130
  279.1 29.3 %pair_correlations.15 = bf16[512,512,128]{2,1,0:T(8,128)(2,1)} custom-call(s32[4]{0:T(128)} %get-tuple-element.27.offs_ref, bf16[128,32,128]{2,1,0:T(8,128)(2,1)} %copy-done.5, bf16[128,32,128]{2,1,0:T(8,128)(2,1)} %copy-done, bf16[128,32,128]{2,1,0:T(8,128)(2,1)} %copy-done.1, ...), custom_call_target="tpu_custom_call", output_to_operand_aliasing={{}: (5, {})} | custom-call | flops 21474836480 | bytes 8388608 | tf_op jit(solution)/shard_map/pair_correlations/pallas_call | solution.py:130
  (16 shorter events, 0.0 us)
Async XLA Ops:
  0.5 1.7 copy-start.7
  3.1 1.2 copy-start.6
  9.2 1.9 collective-permute-start
  11.0 58.0 %copy-start.2 = (bf16[128,32,128]{2,1,0:T(8,128)(2,1)}, bf16[128,32,128]{2,1,0:T(8,128)(2,1)S(1)}, u32[]{:S(2)}) copy-start(bf16[128,32,128]{2,1,0:T(8,128)(2,1)S(1)} %collective-permute-done.refs_0_) | copy-start | bytes 3145732
  11.0 58.0 %collective-permute-start.1 = (bf16[128,32,128]{2,1,0:T(8,128)(2,1)S(1)}, bf16[128,32,128]{2,1,0:T(8,128)(2,1)S(1)}, u32[]{:S(2)}, u32[]{:S(2)}) collective-permute-start(bf16[128,32,128]{2,1,0:T(8,128)(2,1)S(1)} %collective-permute-done.refs_0_), channel_id=1, source_target_pairs={{0,4},{4,0},{8,12},{12,8},{1,5},{5,1},{9,13},{13,9},{2,6},{6,2},{1... | collective-permute-start | bytes 3145736 | tf_op jit(solution)/shard_map/ppermute | solution.py:190
  40.2 59.1 %collective-permute-start.4 = (bf16[128,32,128]{2,1,0:T(8,128)(2,1)}, bf16[128,32,128]{2,1,0:T(8,128)(2,1)}, u32[]{:S(2)}, u32[]{:S(2)}) collective-permute-start(bf16[128,32,128]{2,1,0:T(8,128)(2,1)} %bitcast.10.first_ref), channel_id=1, source_target_pairs={{0,1},{1,2},{2,3},{3,0},{4,5},{5,6},{6,7},{7,4},{8,9},{9,10},{10,1... | collective-permute-start | bytes 3145736 | tf_op jit(solution)/shard_map/ppermute | solution.py:193
  40.2 59.1 %collective-permute-start.2 = (bf16[128,32,128]{2,1,0:T(8,128)(2,1)S(1)}, bf16[128,32,128]{2,1,0:T(8,128)(2,1)S(1)}, u32[]{:S(2)}, u32[]{:S(2)}) collective-permute-start(bf16[128,32,128]{2,1,0:T(8,128)(2,1)S(1)} %collective-permute-done.refs_0_), channel_id=1, source_target_pairs={{0,8},{4,12},{8,0},{12,4},{1,9},{5,13},{9,1},{13,5},{2,10},{6,14},... | collective-permute-start | bytes 3145736 | tf_op jit(solution)/shard_map/ppermute | solution.py:190
  69.1 1.0 copy-start.3
  99.3 29.5 %copy-start = (bf16[128,32,128]{2,1,0:T(8,128)(2,1)}, bf16[128,32,128]{2,1,0:T(8,128)(2,1)S(1)}, u32[]{:S(2)}) copy-start(bf16[128,32,128]{2,1,0:T(8,128)(2,1)S(1)} %collective-permute-done.2.refs_0_) | copy-start | bytes 3145732
  99.4 29.5 %collective-permute-start.3 = (bf16[128,32,128]{2,1,0:T(8,128)(2,1)S(1)}, bf16[128,32,128]{2,1,0:T(8,128)(2,1)S(1)}, u32[]{:S(2)}, u32[]{:S(2)}) collective-permute-start(bf16[128,32,128]{2,1,0:T(8,128)(2,1)S(1)} %collective-permute-done.2.refs_0_), channel_id=1, source_target_pairs={{0,4},{4,0},{8,12},{12,8},{1,5},{5,1},{9,13},{13,9},{2,6},{6,2},{1... | collective-permute-start | bytes 3145736 | tf_op jit(solution)/shard_map/ppermute | solution.py:190
  99.4 59.7 %collective-permute-start.5 = (bf16[128,32,128]{2,1,0:T(8,128)(2,1)}, bf16[128,32,128]{2,1,0:T(8,128)(2,1)S(1)}, u32[]{:S(2)}, u32[]{:S(2)}) collective-permute-start(bf16[128,32,128]{2,1,0:T(8,128)(2,1)} %collective-permute-done.4.first_ref), channel_id=1, source_target_pairs={{0,1},{1,2},{2,3},{3,0},{4,5},{5,6},{6,7},{7,4},{8,9},{9,10},{10,1... | collective-permute-start | bytes 3145736 | tf_op jit(solution)/shard_map/ppermute | solution.py:193
  128.9 1.0 copy-start.1
  159.1 31.1 %copy-start.4 = (bf16[128,32,128]{2,1,0:T(8,128)(2,1)}, bf16[128,32,128]{2,1,0:T(8,128)(2,1)S(1)}, u32[]{:S(2)}) copy-start(bf16[128,32,128]{2,1,0:T(8,128)(2,1)S(1)} %collective-permute-done.5.first_ref) | copy-start | bytes 3145732
  159.1 60.4 %collective-permute-start.6 = (bf16[128,32,128]{2,1,0:T(8,128)(2,1)S(1)}, bf16[128,32,128]{2,1,0:T(8,128)(2,1)S(1)}, u32[]{:S(2)}, u32[]{:S(2)}) collective-permute-start(bf16[128,32,128]{2,1,0:T(8,128)(2,1)S(1)} %collective-permute-done.5.first_ref), channel_id=1, source_target_pairs={{0,1},{1,2},{2,3},{3,0},{4,5},{5,6},{6,7},{7,4},{8,9},{9,10},{10,1... | collective-permute-start | bytes 3145736 | tf_op jit(solution)/shard_map/ppermute | solution.py:193
  219.5 1.0 copy-start.5

commit v3 on v2

--- a/solution.py
+++ b/solution.py
@@ -160,11 +160,6 @@
     outgoing = whiten_block(picked, clip_mask)
     outgoing = outgoing.reshape(owned, windows, 2, half).transpose(3, 2, 1, 0)
     outgoing = outgoing.reshape(half, 2 * windows, owned)
-    across = lax.ppermute(
-        outgoing,
-        ("row", "col"),
-        [(c * cols + r, r * cols + c) for r in range(rows) for c in range(cols)],
-    )
     tile = owned * cols
     shape = (tile, tile, L)
     row, col = lax.axis_index("row"), lax.axis_index("col")
@@ -176,7 +171,12 @@
         gap = ahead + pair * wide - place * lanes
         return jnp.stack([jnp.int32(v) for v in (place, pair, swap, gap)])
 
-    if owned != LANES or rows & (rows - 1) or rows < 2:
+    if owned != LANES or rows & (rows - 1) or rows < 2 or rows != cols:
+        across = lax.ppermute(
+            outgoing,
+            ("row", "col"),
+            [(c * cols + r, r * cols + c) for r in range(rows) for c in range(cols)],
+        )
         firsts = by_lanes(lax.all_gather(outgoing, "col", axis=0))
         seconds = by_lanes(lax.all_gather(across, "row", axis=0))
         lanes = firsts.shape[-1]
@@ -192,16 +192,30 @@
     def hop(value):
         return lax.ppermute(value, "col", [(c, (c + 1) % cols) for c in range(cols)])
 
-    pairs = {0: (across, flipped(across, 1))}
-    held, _ = lax.optimization_barrier((outgoing, across))
+    def brought(near, source):
+        found = None
+        for away in range(rows // 2):
+            moves = []
+            for c in range(cols):
+                for q in (2 * ((c // 2) ^ near), 2 * ((c // 2) ^ near) + 1):
+                    target = 2 * ((c // 2) ^ away) + q % 2
+                    moves.append((c * cols + q, target * cols + c))
+            here = lax.ppermute(source, ("row", "col"), moves)
+            mine = (row // 2) ^ (col // 2) == away
+            found = here if found is None else jnp.where(mine, here, found)
+        return found
+
+    near = brought(0, outgoing)
+    pairs = {0: (near, flipped(near, 1))}
+    held, _ = lax.optimization_barrier((outgoing, near))
     firsts = {0: outgoing, 1: hop(held)} if cols > 1 else {0: outgoing}
-    fars = {p: flipped(across, 2 * p) for p in range(1, rows // 2)}
+    fars = {p: brought(p, held) for p in range(1, rows // 2)}
     order = [(s, p) for s in range(cols) for p in range(rows // 2)]
-    order.sort(key=lambda sp: (max(sp[0] // 2, sp[1]), sp[0] // 2, sp[1], sp[0]))
+    order.sort(key=lambda sp: (sp[0] // 3, sp[1], sp[0]))
     ready = 1
     for step, (s, p) in enumerate(order):
         if step > 0:
-            if p in fars and p not in pairs or step == 1 and fars:
+            if p in fars and p not in pairs or step == 2 and fars:
                 for q in [q for q in fars if q not in pairs][:1]:
                     prev, far = lax.optimization_barrier((prev, fars[q]))
                     pairs[q] = (far, flipped(far, 1))
@@ -216,8 +230,7 @@
                 ready += 1
                 firsts[ready] = hop(firsts[ready - 1])
         place = (col - s) % cols
-        other = row ^ (2 * p)
-        offs = offsets(place, other // 2, other % 2, 2 * owned, owned)
+        offs = offsets(place, (col // 2) ^ p, row % 2, 2 * owned, owned)
         prev = correlate(prev, firsts[s], pairs[p], table, offs, shape)
     return prev
 

time: 309 us -> 366 us (1.18)
  waiting for transfers between devices: 0.02 us -> 96 us
  starting transfers between devices: 57.1 us -> 14.6 us
    ppermute x1 -> x4, waiting for transfers between devices: 0.01 us -> 95.9 us  [brought(): here = lax.ppermute(source, ('row', 'col'), moves)]
    ppermute x3 -> x2, starting transfers between devices: 53.3 us -> 1.25 us  [flipped(): return lax.ppermute(value, 'row', [(r, r ^ bit) for r in range(rows)])]
    ppermute x1 -> x4, starting transfers between devices: 1.87 us -> 9.73 us  [brought(): here = lax.ppermute(source, ('row', 'col'), moves)]
  transfers between devices with their start and end apart: 7 -> 9, of which waited for: 0 -> 2; matrix products, arithmetic and copies ran while one was open for 2% -> 2% of each run, Pallas kernels for 48% -> 48%
where the time goes in v3:
time: 366 us; the launch traced here: 365 us
  Pallas kernels  234 us (64%)
  waiting for transfers between devices  96 us (26%)
  starting transfers between devices  14.6 us (4%)
  local copies, waits for them, and re-layouts  9.23 us (3%)
  other arithmetic  8.22 us (2%)
    pallas_call x8, Pallas kernels, correlate(): pl.pallas_call(functools.partial(pair_kernel, groups), grid_spec=spec, ou...  234 us
    ppermute x4, waiting for transfers between devices, brought(): here = lax.ppermute(source, ('row', 'col'), moves)  95.9 us
    ppermute x4, starting transfers between devices, brought(): here = lax.ppermute(source, ('row', 'col'), moves)  9.73 us
  transfers between devices with their start and end apart: 9, of which 2 were waited for; matrix products, arithmetic and copies ran while one was open for 2% of the time, Pallas kernels for 48%

profile of v3, /device:TPU:0, one launch (start us, length us, event | category | flops | bytes accessed | tf_op | source)
XLA Modules:
  0.0 365.1 jit_solution(4865823243060961204)
XLA Ops:
  0.0 0.5 fusion.18
  0.6 1.7 fusion.30
  2.3 0.1 broadcast_in_dim.28
  2.4 0.1 broadcast_in_dim.29
  2.5 0.6 bitcast_select_fusion
  3.1 1.0 fusion.3
  4.1 0.2 fusion.7
  4.3 0.1 copy.12
  4.4 0.1 convert_element_type.30
  4.5 1.4 multiply_convert_fusion.1
  5.9 0.1 pad_maximum_fusion
  6.0 0.5 copy.13
  6.5 0.3 convert_element_type.31
  6.8 2.3 copy.14
  9.1 4.9 %collective-permute-start = (bf16[128,32,128]{2,1,0:T(8,128)(2,1)}, bf16[128,32,128]{2,1,0:T(8,128)(2,1)S(1)}, u32[]{:S(2)}, u32[]{:S(2)}) collective-permute-start(bf16[128,32,128]{2,1,0:T(8,128)(2,1)} %bitcast.13.first_ref), channel_id=1, source_target_pairs={{0,8},{1,12},{4,9},{5,13},{10,2},{11,6},{14,3},{15,7},{16,24},{17,... | collective-permute-start | bytes 3145736 | tf_op jit(solution)/shard_map/ppermute | solution.py:203
  14.1 1.9 collective-permute-start.1
  15.9 21.9 %collective-permute-done = bf16[128,32,128]{2,1,0:T(8,128)(2,1)S(1)} collective-permute-done((bf16[128,32,128]{2,1,0:T(8,128)(2,1)}, bf16[128,32,128]{2,1,0:T(8,128)(2,1)S(1)}, u32[]{:S(2)}, u32[]{:S(2)}) %collective-permute-start) | collective-permute-done | bytes 1048608 | tf_op jit(solution)/shard_map/ppermute | solution.py:203
  37.8 0.1 broadcast_select_fusion.1.refs_0_
  38.0 1.2 collective-permute-start.2
  39.1 0.6 pad_add_fusion.2.offs_ref
  39.8 0.7 pad_add_fusion.3.offs_ref
  40.4 0.6 pad_add_fusion.7.offs_ref
  41.1 0.6 pad_add_fusion.6.offs_ref
  41.7 0.6 pad_add_fusion.1.offs_ref
  42.3 0.6 pad_add_fusion.5.offs_ref
  42.9 0.7 pad_add_fusion
  43.5 0.3 multiply_convert_fusion.3
  43.9 0.6 maximum_bitcast_fusion.refs_2_
  44.5 1.9 collective-permute-start.3
  46.4 1.6 collective-permute-start.5
  48.0 1.3 collective-permute-start.6
  49.4 1.0 copy-done.3
  50.3 29.3 %pair_correlations.8.refs_3_ = bf16[512,512,128]{2,1,0:T(8,128)(2,1)} custom-call(s32[4]{0:T(128)} %pad_add_fusion.2.offs_ref, bf16[128,32,128]{2,1,0:T(8,128)(2,1)} %bitcast.13.first_ref, bf16[128,32,128]{2,1,0:T(8,128)(2,1)} %copy-done.2, bf16[128,32,128]{2,1,0:T(8,128)(2,1)} %copy-done.3, bf16[128,256]{1,0:T(8,128)(2,1)} %maximum_bitcast_fusion.refs_2_), custom_call_target="tpu_custom_call" | custom-call | flops 21474836480 | bytes 8388608 | tf_op jit(solution)/shard_map/pair_correlations/pallas_call | solution.py:130
  79.6 1.2 collective-permute-start.4
  80.8 29.3 %pair_correlations.9.refs_3_ = bf16[512,512,128]{2,1,0:T(8,128)(2,1)} custom-call(s32[4]{0:T(128)} %pad_add_fusion.3.offs_ref, bf16[128,32,128]{2,1,0:T(8,128)(2,1)} %collective-permute-done.3.first_ref, bf16[128,32,128]{2,1,0:T(8,128)(2,1)} %copy-done.2, bf16[128,32,128]{2,1,0:T(8,128)(2,1)} %copy-done.3, ...), custom_call_target="tpu_custom_call", output_to_operand_aliasing={{}: (5, {})} | custom-call | flops 21474836480 | bytes 8388608 | tf_op jit(solution)/shard_map/pair_correlations/pallas_call | solution.py:130
  110.1 74.0 %collective-permute-done.6 = bf16[128,32,128]{2,1,0:T(8,128)(2,1)} collective-permute-done((bf16[128,32,128]{2,1,0:T(8,128)(2,1)}, bf16[128,32,128]{2,1,0:T(8,128)(2,1)}, u32[]{:S(2)}, u32[]{:S(2)}) %collective-permute-start.6) | collective-permute-done | bytes 1048608 | tf_op jit(solution)/shard_map/ppermute | solution.py:203
  184.2 1.3 broadcast_select_fusion.refs_0_
  185.5 0.1 collective-permute-start.8
  185.6 1.1 copy-done.4
  186.7 29.3 %pair_correlations.10.refs_3_ = bf16[512,512,128]{2,1,0:T(8,128)(2,1)} custom-call(s32[4]{0:T(128)} %pad_add_fusion.1.offs_ref, bf16[128,32,128]{2,1,0:T(8,128)(2,1)} %copy-done.4, bf16[128,32,128]{2,1,0:T(8,128)(2,1)} %copy-done.2, bf16[128,32,128]{2,1,0:T(8,128)(2,1)} %copy-done.3, ...), custom_call_target="tpu_custom_call", output_to_operand_aliasing={{}: (5, {})} | custom-call | flops 21474836480 | bytes 8388608 | tf_op jit(solution)/shard_map/pair_correlations/pallas_call | solution.py:130
  216.0 0.6 collective-permute-start.7
  216.6 1.0 copy-done.1
  217.6 29.3 %pair_correlations.11.refs_3_ = bf16[512,512,128]{2,1,0:T(8,128)(2,1)} custom-call(s32[4]{0:T(128)} %pad_add_fusion.7.offs_ref, bf16[128,32,128]{2,1,0:T(8,128)(2,1)} %bitcast.13.first_ref, bf16[128,32,128]{2,1,0:T(8,128)(2,1)} %copy-done, bf16[128,32,128]{2,1,0:T(8,128)(2,1)} %copy-done.1, ...), custom_call_target="tpu_custom_call", output_to_operand_aliasing={{}: (5, {})} | custom-call | flops 21474836480 | bytes 8388608 | tf_op jit(solution)/shard_map/pair_correlations/pallas_call | solution.py:130
  246.9 29.3 %pair_correlations.12.refs_3_ = bf16[512,512,128]{2,1,0:T(8,128)(2,1)} custom-call(s32[4]{0:T(128)} %pad_add_fusion.6.offs_ref, bf16[128,32,128]{2,1,0:T(8,128)(2,1)} %collective-permute-done.3.first_ref, bf16[128,32,128]{2,1,0:T(8,128)(2,1)} %copy-done, bf16[128,32,128]{2,1,0:T(8,128)(2,1)} %copy-done.1, ...), custom_call_target="tpu_custom_call", output_to_operand_aliasing={{}: (5, {})} | custom-call | flops 21474836480 | bytes 8388608 | tf_op jit(solution)/shard_map/pair_correlations/pallas_call | solution.py:130
  276.2 29.3 %pair_correlations.13.refs_3_ = bf16[512,512,128]{2,1,0:T(8,128)(2,1)} custom-call(s32[4]{0:T(128)} %pad_add_fusion.5.offs_ref, bf16[128,32,128]{2,1,0:T(8,128)(2,1)} %copy-done.4, bf16[128,32,128]{2,1,0:T(8,128)(2,1)} %copy-done, bf16[128,32,128]{2,1,0:T(8,128)(2,1)} %copy-done.1, ...), custom_call_target="tpu_custom_call", output_to_operand_aliasing={{}: (5, {})} | custom-call | flops 21474836480 | bytes 8388608 | tf_op jit(solution)/shard_map/pair_correlations/pallas_call | solution.py:130
  305.5 1.0 copy-done.5
  306.5 29.3 %pair_correlations.14.refs_3_ = bf16[512,512,128]{2,1,0:T(8,128)(2,1)} custom-call(s32[4]{0:T(128)} %get-tuple-element.28.offs_ref, bf16[128,32,128]{2,1,0:T(8,128)(2,1)} %copy-done.5, bf16[128,32,128]{2,1,0:T(8,128)(2,1)} %copy-done.2, bf16[128,32,128]{2,1,0:T(8,128)(2,1)} %copy-done.3, ...), custom_call_target="tpu_custom_call", output_to_operand_aliasing={{}: (5, {})} | custom-call | flops 21474836480 | bytes 8388608 | tf_op jit(solution)/shard_map/pair_correlations/pallas_call | solution.py:130
  335.8 29.3 %pair_correlations.15 = bf16[512,512,128]{2,1,0:T(8,128)(2,1)} custom-call(s32[4]{0:T(128)} %get-tuple-element.27.offs_ref, bf16[128,32,128]{2,1,0:T(8,128)(2,1)} %copy-done.5, bf16[128,32,128]{2,1,0:T(8,128)(2,1)} %copy-done, bf16[128,32,128]{2,1,0:T(8,128)(2,1)} %copy-done.1, ...), custom_call_target="tpu_custom_call", output_to_operand_aliasing={{}: (5, {})} | custom-call | flops 21474836480 | bytes 8388608 | tf_op jit(solution)/shard_map/pair_correlations/pallas_call | solution.py:130
  (23 shorter events, 0.1 us)
Async XLA Ops:
  0.5 1.7 copy-start.7
  3.1 1.2 copy-start.6
  9.1 28.7 %collective-permute-start = (bf16[128,32,128]{2,1,0:T(8,128)(2,1)}, bf16[128,32,128]{2,1,0:T(8,128)(2,1)S(1)}, u32[]{:S(2)}, u32[]{:S(2)}) collective-permute-start(bf16[128,32,128]{2,1,0:T(8,128)(2,1)} %bitcast.13.first_ref), channel_id=1, source_target_pairs={{0,8},{1,12},{4,9},{5,13},{10,2},{11,6},{14,3},{15,7},{16,24},{17,... | collective-permute-start | bytes 3145736 | tf_op jit(solution)/shard_map/ppermute | solution.py:203
  14.1 23.8 %collective-permute-start.1 = (bf16[128,32,128]{2,1,0:T(8,128)(2,1)}, bf16[128,32,128]{2,1,0:T(8,128)(2,1)S(1)}, u32[]{:S(2)}, u32[]{:S(2)}) collective-permute-start(bf16[128,32,128]{2,1,0:T(8,128)(2,1)} %bitcast.13.first_ref), channel_id=1, source_target_pairs={{0,0},{1,4},{4,1},{5,5},{10,10},{11,14},{14,11},{15,15},{16,16},{1... | collective-permute-start | bytes 3145736 | tf_op jit(solution)/shard_map/ppermute | solution.py:203
  38.0 11.4 %copy-start.2 = (bf16[128,32,128]{2,1,0:T(8,128)(2,1)}, bf16[128,32,128]{2,1,0:T(8,128)(2,1)S(1)}, u32[]{:S(2)}) copy-start(bf16[128,32,128]{2,1,0:T(8,128)(2,1)S(1)} %broadcast_select_fusion.1.refs_0_) | copy-start | bytes 3145732
  38.0 11.4 %collective-permute-start.2 = (bf16[128,32,128]{2,1,0:T(8,128)(2,1)S(1)}, bf16[128,32,128]{2,1,0:T(8,128)(2,1)S(1)}, u32[]{:S(2)}, u32[]{:S(2)}) collective-permute-start(bf16[128,32,128]{2,1,0:T(8,128)(2,1)S(1)} %broadcast_select_fusion.1.refs_0_), channel_id=1, source_target_pairs={{0,4},{4,0},{8,12},{12,8},{1,5},{5,1},{9,13},{13,9},{2,6},{6,2},{1... | collective-permute-start | bytes 3145736 | tf_op jit(solution)/shard_map/ppermute | solution.py:190
  44.5 35.1 %collective-permute-start.3 = (bf16[128,32,128]{2,1,0:T(8,128)(2,1)}, bf16[128,32,128]{2,1,0:T(8,128)(2,1)}, u32[]{:S(2)}, u32[]{:S(2)}) collective-permute-start(bf16[128,32,128]{2,1,0:T(8,128)(2,1)} %bitcast.13.first_ref), channel_id=1, source_target_pairs={{0,1},{1,2},{2,3},{3,0},{4,5},{5,6},{6,7},{7,4},{8,9},{9,10},{10,1... | collective-permute-start | bytes 3145736 | tf_op jit(solution)/shard_map/ppermute | solution.py:193
  46.4 63.7 %collective-permute-start.5 = (bf16[128,32,128]{2,1,0:T(8,128)(2,1)}, bf16[128,32,128]{2,1,0:T(8,128)(2,1)}, u32[]{:S(2)}, u32[]{:S(2)}) collective-permute-start(bf16[128,32,128]{2,1,0:T(8,128)(2,1)} %bitcast.13.first_ref), channel_id=1, source_target_pairs={{2,8},{3,12},{6,9},{7,13},{8,2},{9,6},{12,3},{13,7},{18,24},{19,28... | collective-permute-start | bytes 3145736 | tf_op jit(solution)/shard_map/ppermute | solution.py:203
  48.0 136.1 %collective-permute-start.6 = (bf16[128,32,128]{2,1,0:T(8,128)(2,1)}, bf16[128,32,128]{2,1,0:T(8,128)(2,1)}, u32[]{:S(2)}, u32[]{:S(2)}) collective-permute-start(bf16[128,32,128]{2,1,0:T(8,128)(2,1)} %bitcast.13.first_ref), channel_id=1, source_target_pairs={{2,0},{3,4},{6,1},{7,5},{8,10},{9,14},{12,11},{13,15},{18,16},{19,... | collective-permute-start | bytes 3145736 | tf_op jit(solution)/shard_map/ppermute | solution.py:203
  49.4 1.0 copy-start.3
  79.6 106.0 %collective-permute-start.4 = (bf16[128,32,128]{2,1,0:T(8,128)(2,1)}, bf16[128,32,128]{2,1,0:T(8,128)(2,1)S(1)}, u32[]{:S(2)}, u32[]{:S(2)}) collective-permute-start(bf16[128,32,128]{2,1,0:T(8,128)(2,1)} %collective-permute-done.3.first_ref), channel_id=1, source_target_pairs={{0,1},{1,2},{2,3},{3,0},{4,5},{5,6},{6,7},{7,4},{8,9},{9,10},{10,1... | collective-permute-start | bytes 3145736 | tf_op jit(solution)/shard_map/ppermute | solution.py:193
  185.5 30.5 %copy-start = (bf16[128,32,128]{2,1,0:T(8,128)(2,1)}, bf16[128,32,128]{2,1,0:T(8,128)(2,1)S(1)}, u32[]{:S(2)}) copy-start(bf16[128,32,128]{2,1,0:T(8,128)(2,1)S(1)} %broadcast_select_fusion.refs_0_) | copy-start | bytes 3145732
  185.5 31.1 %collective-permute-start.8 = (bf16[128,32,128]{2,1,0:T(8,128)(2,1)S(1)}, bf16[128,32,128]{2,1,0:T(8,128)(2,1)S(1)}, u32[]{:S(2)}, u32[]{:S(2)}) collective-permute-start(bf16[128,32,128]{2,1,0:T(8,128)(2,1)S(1)} %broadcast_select_fusion.refs_0_), channel_id=1, source_target_pairs={{0,4},{4,0},{8,12},{12,8},{1,5},{5,1},{9,13},{13,9},{2,6},{6,2},{1... | collective-permute-start | bytes 3145736 | tf_op jit(solution)/shard_map/ppermute | solution.py:190
  185.6 1.1 copy-start.4
  216.0 89.5 %collective-permute-start.7 = (bf16[128,32,128]{2,1,0:T(8,128)(2,1)}, bf16[128,32,128]{2,1,0:T(8,128)(2,1)S(1)}, u32[]{:S(2)}, u32[]{:S(2)}) collective-permute-start(bf16[128,32,128]{2,1,0:T(8,128)(2,1)} %copy-done.4), channel_id=1, source_target_pairs={{0,1},{1,2},{2,3},{3,0},{4,5},{5,6},{6,7},{7,4},{8,9},{9,10},{10,1... | collective-permute-start | bytes 3145736 | tf_op jit(solution)/shard_map/ppermute | solution.py:193
  216.6 1.0 copy-start.1
  305.5 1.0 copy-start.5
